TPU v7x, 32 devices: a whole 2x2x4 slice. The times are simulated.
32 devices in a mesh: chan: 8 (over y, x, core), sub: 4 (over z).
Axes of the slice: x: 2, y: 2, z: 4, core: 2. Of those that a mesh axis runs over, the one named last changes fastest.
Arguments:
- spectra: bfloat16 [4, 2, 512, 32768], P('sub', None, None, 'chan'), may hold values from -12 to 12
- filter_init: float32 [2, 32768], P(None, 'chan'), may hold values from -2.1 to 2.1
- profile_init: float32 [2, 512], replicated, may hold values from -1.4 to 1.4
Outputs:
- filter_out: float32 [2, 32768], P(None, 'chan')
- profile_out: float32 [2, 512], replicated
- misfit: float32 [1], replicated
All inputs are finite; a program needn't handle non-finite values.
Results may differ from a plain program's by a relative error of at most 0.0003.
Values sent between devices are 32-bit elements; how exact they have to be, the bound alone decides.
A program may use at most 192 MiB of HBM per device.

v0:
```python
import functools

import jax
import jax.numpy as jnp
from jax import lax
from jax.experimental import pallas as pl
from jax.experimental.pallas import tpu as pltpu
from jax.sharding import PartitionSpec as P

filter_rate = 0.1
profile_rate = 0.1
epsilon = 1e-06
LANES = 128
MESH = pl.DeviceIdType.MESH
F32 = jnp.float32


def lanes_of(shape):
    return lax.broadcasted_iota(jnp.int32, shape, len(shape) - 1)


def shift_right(x, k):
    rolled = pltpu.roll(x, k, 2)
    before = jnp.concatenate([rolled[-1:], rolled[:-1]], axis=0)
    return jnp.where(lanes_of(x.shape) >= k, rolled, before)


def shift_left(x, k):
    rolled = pltpu.roll(x, LANES - k, 2)
    after = jnp.concatenate([rolled[1:], rolled[:1]], axis=0)
    return jnp.where(lanes_of(x.shape) < LANES - k, rolled, after)


def by_sublane(x, shift):
    sub = lax.broadcasted_iota(jnp.int32, x.shape, 1)
    for k in (1, 2, 4):
        x = jnp.where((sub & k) != 0, shift(x, k), x)
    return x


def gradient_kernel(
    nb, na, factor, f_ref, q_ref, x_ref, main_ref, tail_ref, head_ref,
    base_f, base_b, fwd, bwd, up, lo, up_all, lo_all, prof_acc, err_acc,
):
    m = pl.program_id(0)
    ext = nb + na
    tile = (8, LANES)

    @pl.when(m == 0)
    def _():
        for ri in range(2):
            high = jnp.broadcast_to(f_ref[ri, na:, :][:, None, :], (ext, 8, LANES))
            base_f[ri] = by_sublane(high, shift_left)
            low = jnp.broadcast_to(f_ref[ri, :ext, :][:, None, :], (ext, 8, LANES))
            base_b[ri] = by_sublane(low, shift_right)
        up_all[...] = jnp.zeros_like(up_all)
        lo_all[...] = jnp.zeros_like(lo_all)
        err_acc[...] = jnp.zeros_like(err_acc)

    lane = lanes_of(tile)
    for g in range(2):
        t = 16 * m + 8 * g
        left = lax.rem(LANES - t, LANES)
        rows = slice(8 * g, 8 * g + 8)
        for ri in range(2):
            now = pltpu.roll(base_f[ri, 0], left, 1)
            for n in range(ext - 1):
                after = pltpu.roll(base_f[ri, n + 1], left, 1)
                fwd[ri, n, rows] = jnp.where(lane < LANES - t, now, after)
                now = after
            before = pltpu.roll(base_b[ri, 0], t, 1)
            for n in range(1, ext):
                now = pltpu.roll(base_b[ri, n], t, 1)
                bwd[ri, n, rows] = jnp.where(lane >= t, now, before)
                before = now

    for ri in range(2):
        for n in range(na - 1):
            up[ri, nb + n] = jnp.zeros((16, LANES), F32)
            lo[ri, n] = jnp.zeros((16, LANES), F32)

    for a in range(na):
        qr = q_ref[0, a]
        qi = q_ref[1, a]

        def body(b, carry, a=a, qr=qr, qi=qi):
            gr, gi, er = carry
            cols = pl.ds(pl.multiple_of(b * LANES, LANES), LANES)
            xr = x_ref[0, a, :, cols].astype(F32)
            xi = x_ref[1, a, :, cols].astype(F32)
            fr, fi = fwd[0, b + a], fwd[1, b + a]
            br, bi = bwd[0, b - a + na], bwd[1, b - a + na]
            pr = fr * br + fi * bi
            pi = fi * br - fr * bi
            rr = xr - (pr * qr - pi * qi)
            ri = xi - (pr * qi + pi * qr)
            er = er + (rr * rr + ri * ri)
            gr = gr + (rr * pr + ri * pi)
            gi = gi + (ri * pr - rr * pi)
            yr = rr * qr + ri * qi
            yi = ri * qr - rr * qi
            ur = yr * br - yi * bi
            ui = yr * bi + yi * br
            vr = yr * fr + yi * fi
            vi = yr * fi - yi * fr
            iu, il = b + a, b - a + na - 1
            if a == 0:
                up[0, iu] = ur
                up[1, iu] = ui
                lo[0, il] = vr
                lo[1, il] = vi
            else:
                up[0, iu] = up[0, iu] + ur
                up[1, iu] = up[1, iu] + ui
                lo[0, il] = lo[0, il] + vr
                lo[1, il] = lo[1, il] + vi
            return gr, gi, er

        zero = jnp.zeros((16, LANES), F32)
        gr, gi, er = lax.fori_loop(0, nb, body, (zero, zero, zero), unroll=2)
        rows = pl.ds(pl.multiple_of(16 * m, 16), 16)
        prof_acc[0, a, rows] = gr
        prof_acc[1, a, rows] = gi
        err_acc[...] = err_acc[...] + er

    zero8 = jnp.zeros(tile, F32)
    for g in range(2):
        t = 16 * m + 8 * g
        left = lax.rem(LANES - t, LANES)
        rows = slice(8 * g, 8 * g + 8)
        for ri in range(2):
            before = zero8
            for n in range(ext):
                now = pltpu.roll(up[ri, n, rows], t, 1) if n < ext - 1 else zero8
                up_all[ri, n] = up_all[ri, n] + jnp.where(lane >= t, now, before)
                before = now
            before = zero8
            for n in range(ext):
                now = pltpu.roll(lo[ri, n, rows], left, 1) if n < ext - 1 else zero8
                lo_all[ri, n] = lo_all[ri, n] + jnp.where(lane < LANES - t, before, now)
                before = now

    @pl.when(m == pl.num_programs(0) - 1)
    def _():
        for ri in range(2):
            upper = factor * jnp.sum(by_sublane(up_all[ri], shift_right), axis=1)
            lower = factor * jnp.sum(by_sublane(lo_all[ri], shift_left), axis=1)
            main_ref[ri * nb : (ri + 1) * nb] = upper[:nb] + lower[na:]
            tail_ref[ri * na : (ri + 1) * na] = upper[nb:]
            head_ref[ri * na : (ri + 1) * na] = lower[:na]
            for a in range(na):
                sums = lax.dot_general(
                    jnp.ones(tile, F32), prof_acc[ri, a], (((1,), (1,)), ((), ())),
                    precision=lax.Precision.HIGHEST, preferred_element_type=F32,
                )
                row = 2 * nb + ri * na + a
                main_ref[row : row + 1] = factor * sums[:1]
        main_ref[2 * nb + 2 * na : 2 * nb + 2 * na + 1] = jnp.sum(
            err_acc[...], axis=0, keepdims=True
        )


def reduce_kernel(
    nb, na, n_chan, n_sub, harmonics, weight, f_ref, q_ref, main_ref, tail_ref, head_ref,
    out_ref, prof_ref, misfit_ref,
    mains, tails, heads, packs, pack,
    s_main, r_main, s_tail, r_tail, s_head, r_head, s_pack, r_pack,
):
    chan = lax.axis_index("chan")
    sub = lax.axis_index("sub")
    above = lax.rem(chan + 1, n_chan)
    below = lax.rem(chan + n_chan - 1, n_chan)

    barrier = pltpu.get_barrier_semaphore()
    greeted = 0
    for off in range(n_sub):
        peer = lax.rem(sub + off, n_sub)
        for c in (above, below) + ((chan,) if off else ()):
            pl.semaphore_signal(barrier, inc=1, device_id=(c, peer), device_id_type=MESH)
            greeted += 1
    for off in range(2, n_chan - 1):
        pl.semaphore_signal(
            barrier, inc=1, device_id=(lax.rem(chan + off, n_chan), sub), device_id_type=MESH
        )
        greeted += 1
    pl.semaphore_wait(barrier, greeted)

    def copy_to(src, dst, send, recv, device):
        return pltpu.make_async_remote_copy(
            src_ref=src, dst_ref=dst, send_sem=send, recv_sem=recv,
            device_id=device, device_id_type=MESH,
        )

    sends = []
    for off in range(1, n_sub):
        peer = lax.rem(sub + off, n_sub)
        sends.append(
            copy_to(main_ref, mains.at[sub], s_main.at[off], r_main.at[sub], (chan, peer))
        )
    for off in range(n_sub):
        peer = lax.rem(sub + off, n_sub)
        sends.append(
            copy_to(tail_ref, tails.at[sub], s_tail.at[off], r_tail.at[sub], (above, peer))
        )
        sends.append(
            copy_to(head_ref, heads.at[sub], s_head.at[off], r_head.at[sub], (below, peer))
        )
    for copy in sends:
        copy.start()
    mains[sub] = main_ref[...]
    for off in range(n_sub):
        peer = lax.rem(sub + off, n_sub)
        if off:
            copy_to(
                main_ref, mains.at[peer], s_main.at[off], r_main.at[peer], (chan, peer)
            ).wait_recv()
        copy_to(
            tail_ref, tails.at[peer], s_tail.at[off], r_tail.at[peer], (above, peer)
        ).wait_recv()
        copy_to(
            head_ref, heads.at[peer], s_head.at[off], r_head.at[peer], (below, peer)
        ).wait_recv()

    total = mains[0]
    tail = tails[0]
    head = heads[0]
    for s in range(1, n_sub):
        total = total + mains[s]
        tail = tail + tails[s]
        head = head + heads[s]
    tail = jnp.where(chan > 0, tail, 0.0)
    head = jnp.where(chan < n_chan - 1, head, 0.0)
    grads = []
    squares = jnp.zeros((1, LANES), F32)
    for ri in range(2):
        own = total[ri * nb : (ri + 1) * nb]
        part = slice(ri * na, (ri + 1) * na)
        grad = jnp.concatenate([own[:na] + tail[part], own[na:]], axis=0)
        grad = jnp.concatenate([grad[: nb - na], grad[nb - na :] + head[part]], axis=0)
        squares = squares + jnp.sum(grad * grad, axis=0, keepdims=True)
        grads.append(grad)
    prof_rows = 2 * na
    pack[...] = jnp.zeros_like(pack)
    pack[: prof_rows + 1] = total[2 * nb : 2 * nb + prof_rows + 1]
    pack[prof_rows + 1 : prof_rows + 2] = squares
    packs[chan] = pack[...]

    for copy in sends:
        copy.wait_send()
    exchanges = []
    for off in range(1, n_chan):
        peer = lax.rem(chan + off, n_chan)
        exchanges.append(
            copy_to(pack, packs.at[chan], s_pack.at[off], r_pack.at[chan], (peer, sub))
        )
    for copy in exchanges:
        copy.start()
    for off in range(1, n_chan):
        peer = lax.rem(chan + off, n_chan)
        copy_to(pack, packs.at[peer], s_pack.at[off], r_pack.at[peer], (peer, sub)).wait_recv()
    sums = packs[0]
    for c in range(1, n_chan):
        sums = sums + packs[c]
    prof_grad = sums[:prof_rows]
    error = jnp.sum(sums[prof_rows : prof_rows + 1])
    square = jnp.sum(sums[prof_rows + 1 : prof_rows + 2], axis=1, keepdims=True)
    channels = n_chan * nb * LANES
    misfit_ref[0] = error * (weight / channels)
    scale = filter_rate / jnp.sqrt(square / (2 * channels) + epsilon)
    for ri in range(2):
        step = grads[ri] * scale
        for n in range(nb):
            cols = slice(n * LANES, (n + 1) * LANES)
            out_ref[ri : ri + 1, cols] = f_ref[ri : ri + 1, cols] - step[n : n + 1]
    mean = jnp.sum(prof_grad * prof_grad, keepdims=True) / (2 * harmonics)
    prof_step = prof_grad * (profile_rate / jnp.sqrt(mean + epsilon))
    for ri in range(2):
        for a in range(na):
            cols = slice(a * LANES, (a + 1) * LANES)
            row = ri * na + a
            prof_ref[ri : ri + 1, cols] = q_ref[ri : ri + 1, cols] - prof_step[row : row + 1]
    for copy in exchanges:
        copy.wait_send()


def on_device(spectra, filter_init, profile_init):
    harmonics = profile_init.shape[1]
    owned = filter_init.shape[1]
    n_chan = lax.axis_size("chan")
    n_sub = lax.axis_size("sub")
    nb = owned // LANES
    na = harmonics // LANES
    ext = nb + na
    weight = 1.0 / (n_sub * spectra.shape[0] * harmonics)
    factor = -2.0 * weight
    main_rows = 2 * nb + 2 * na + 8

    low = lax.ppermute(
        filter_init[:, owned - harmonics :], "chan", [(i, i + 1) for i in range(n_chan - 1)]
    )
    high = lax.ppermute(
        filter_init[:, :harmonics], "chan", [(i + 1, i) for i in range(n_chan - 1)]
    )
    padded = jnp.concatenate([low, filter_init, high], axis=1).reshape(2, nb + 2 * na, LANES)
    prof = jnp.broadcast_to(
        profile_init.reshape(2, na, LANES)[..., None], (2, na, LANES, LANES)
    )
    x = spectra.reshape(2, na, LANES, owned)

    whole = pl.BlockSpec(memory_space=pltpu.VMEM)
    main, tail, head = pl.pallas_call(
        functools.partial(gradient_kernel, nb, na, factor),
        grid=(LANES // 16,),
        in_specs=[
            pl.BlockSpec((2, nb + 2 * na, LANES), lambda m: (0, 0, 0)),
            pl.BlockSpec((2, na, 16, LANES), lambda m: (0, 0, m, 0)),
            pl.BlockSpec((2, na, 16, owned), lambda m: (0, 0, m, 0)),
        ],
        out_specs=[
            pl.BlockSpec((main_rows, LANES), lambda m: (0, 0)),
            pl.BlockSpec((2 * na, LANES), lambda m: (0, 0)),
            pl.BlockSpec((2 * na, LANES), lambda m: (0, 0)),
        ],
        out_shape=[
            jax.ShapeDtypeStruct((main_rows, LANES), F32),
            jax.ShapeDtypeStruct((2 * na, LANES), F32),
            jax.ShapeDtypeStruct((2 * na, LANES), F32),
        ],
        scratch_shapes=[
            pltpu.VMEM((2, ext, 8, LANES), F32),
            pltpu.VMEM((2, ext, 8, LANES), F32),
            pltpu.VMEM((2, ext, 16, LANES), F32),
            pltpu.VMEM((2, ext, 16, LANES), F32),
            pltpu.VMEM((2, ext, 16, LANES), F32),
            pltpu.VMEM((2, ext, 16, LANES), F32),
            pltpu.VMEM((2, ext, 8, LANES), F32),
            pltpu.VMEM((2, ext, 8, LANES), F32),
            pltpu.VMEM((2, na, LANES, LANES), F32),
            pltpu.VMEM((16, LANES), F32),
        ],
    )(padded, prof, x)

    dma = pltpu.SemaphoreType.DMA
    return pl.pallas_call(
        functools.partial(reduce_kernel, nb, na, n_chan, n_sub, harmonics, weight),
        in_specs=[whole] * 5,
        out_specs=[whole, whole, pl.BlockSpec(memory_space=pltpu.SMEM)],
        out_shape=[
            jax.ShapeDtypeStruct((2, owned), F32),
            jax.ShapeDtypeStruct((2, harmonics), F32),
            jax.ShapeDtypeStruct((1,), F32),
        ],
        scratch_shapes=[
            pltpu.VMEM((n_sub, main_rows, LANES), F32),
            pltpu.VMEM((n_sub, 2 * na, LANES), F32),
            pltpu.VMEM((n_sub, 2 * na, LANES), F32),
            pltpu.VMEM((n_chan, 2 * na + 8, LANES), F32),
            pltpu.VMEM((2 * na + 8, LANES), F32),
            dma((n_sub,)), dma((n_sub,)),
            dma((n_sub,)), dma((n_sub,)),
            dma((n_sub,)), dma((n_sub,)),
            dma((n_chan,)), dma((n_chan,)),
        ],
        compiler_params=pltpu.CompilerParams(collective_id=0, has_side_effects=True),
    )(filter_init, profile_init, main, tail, head)


def solution(mesh):
    return jax.shard_map(
        on_device,
        mesh=mesh,
        in_specs=(P("sub", None, None, "chan"), P(None, "chan"), P()),
        out_specs=(P(None, "chan"), P(), P()),
        check_vma=False,
    )
```

profile of v0, /device:TPU:0, one launch (start us, length us, event | category | flops | bytes accessed | tf_op | source)
XLA Modules:
  0.0 60.4 jit_solution(12947087630496596604)
XLA Ops:
  0.6 0.7 %fusion = (f32[2,512]{1,0:T(2,128)S(1)}, f32[2,512]{1,0:T(2,128)S(1)}) fusion(f32[2,4096]{1,0:T(2,128)} %f_ref.1), kind=kLoop, calls=%fused_computation.2 | loop fusion | bytes 16384 | tf_op jit(solution)/shard_map/slice | solution.py:299
  1.3 2.4 %collective-permute-start = (f32[2,512]{1,0:T(2,128)S(1)}, f32[2,512]{1,0:T(2,128)S(1)}, u32[]{:S(2)}, u32[]{:S(2)}) collective-permute-start(f32[2,512]{1,0:T(2,128)S(1)} %get-tuple-element.9), channel_id=1, source_target_pairs={{0,4},{4,8},{8,12},{12,16},{16,20},{20,24},{24,28},{1,5},{5,9},{9,... | collective-permute-start | bytes 12296 | tf_op jit(solution)/shard_map/ppermute | solution.py:298
  3.7 1.3 %collective-permute-start.1 = (f32[2,512]{1,0:T(2,128)S(1)}, f32[2,512]{1,0:T(2,128)S(1)}, u32[]{:S(2)}, u32[]{:S(2)}) collective-permute-start(f32[2,512]{1,0:T(2,128)S(1)} %get-tuple-element.10), channel_id=1, source_target_pairs={{4,0},{8,4},{12,8},{16,12},{20,16},{24,20},{28,24},{5,1},{9,5},{13... | collective-permute-start | bytes 12296 | tf_op jit(solution)/shard_map/ppermute | solution.py:301
  5.0 0.7 %broadcast_in_dim.7 = f32[2,4,128]{2,1,0:T(4,128)S(1)} reshape(f32[2,512]{1,0:T(2,128)} %q_ref.1) | data formatting | bytes 8192 | tf_op jit(solution)/shard_map/broadcast_in_dim | solution.py:305
  5.7 0.0 collective-permute-done
  5.7 3.1 %collective-permute-done.1 = f32[2,512]{1,0:T(2,128)S(1)} collective-permute-done((f32[2,512]{1,0:T(2,128)S(1)}, f32[2,512]{1,0:T(2,128)S(1)}, u32[]{:S(2)}, u32[]{:S(2)}) %collective-permute-start.1) | collective-permute-done | bytes 4128 | tf_op jit(solution)/shard_map/ppermute | solution.py:301
  8.9 0.8 %maximum_bitcast_fusion = f32[1,2,40,128]{3,1,2,0:T(2,128)S(1)} fusion(f32[2,512]{1,0:T(2,128)S(1)} %collective-permute-done.1, f32[2,4096]{1,0:T(2,128)} %f_ref.1, f32[2,512]{1,0:T(2,128)S(1)} %collective-permute-done), kind=kLoop, calls=%fused_computation.1 | loop fusion | flops 20480 | bytes 81920
  9.7 0.6 %copy.8 = f32[1,2,40,128]{3,2,1,0:T(8,128)} copy(f32[1,2,40,128]{3,1,2,0:T(2,128)S(1)} %maximum_bitcast_fusion) | data formatting | bytes 81920
  10.3 1.0 %broadcast_in_dim.8.q_ref = f32[2,4,128,128]{3,2,1,0:T(8,128)} broadcast(f32[2,4,128]{2,1,0:T(4,128)S(1)} %broadcast_in_dim.7), dimensions={0,1,2} | broadcast | bytes 528384 | tf_op jit(solution)/shard_map/broadcast_in_dim | solution.py:305
  11.3 26.9 %shard_map.58 = (f32[80,128]{1,0:T(8,128)}, f32[8,128]{1,0:T(8,128)}, f32[8,128]{1,0:T(8,128)}) custom-call(f32[2,40,128]{2,1,0:T(8,128)} %bitcast.7, f32[2,4,128,128]{3,2,1,0:T(8,128)} %broadcast_in_dim.8.q_ref, bf16[2,4,128,4096]{3,2,1,0:T(8,128)(2,1)} %bitcast.6), custom_call_target="tpu_custom_call" | custom-call | tf_op jit(solution)/shard_map/pallas_call | solution.py:311
  38.1 17.9 %shard_map.59 = (f32[2,4096]{1,0:T(2,128)}, f32[2,512]{1,0:T(2,128)}, f32[1]{0:T(128)}) custom-call(f32[2,4096]{1,0:T(2,128)} %f_ref.1, f32[2,512]{1,0:T(2,128)} %q_ref.1, f32[80,128]{1,0:T(8,128)} %get-tuple-element.6.main_ref, f32[8,128]{1,0:T(8,128)} %get-tuple-element.7.tail_ref, f32[8,128]{1,0:T(8,128)} %get-tuple-element.8.head_ref), custom_call_target="tpu_custom_call" | custom-call | tf_op jit(solution)/shard_map/pallas_call | solution.py:344
  56.0 1.4 %copy.12 = f32[2,4096]{1,0:T(2,128)} copy(f32[2,4096]{1,0:T(2,128)} %get-tuple-element.14) | data formatting | bytes 65536
  57.4 1.3 %copy.13 = f32[2,512]{1,0:T(2,128)} copy(f32[2,512]{1,0:T(2,128)} %get-tuple-element.15) | data formatting | bytes 8192
Async XLA Ops:
  1.3 4.4 %collective-permute-start = (f32[2,512]{1,0:T(2,128)S(1)}, f32[2,512]{1,0:T(2,128)S(1)}, u32[]{:S(2)}, u32[]{:S(2)}) collective-permute-start(f32[2,512]{1,0:T(2,128)S(1)} %get-tuple-element.9), channel_id=1, source_target_pairs={{0,4},{4,8},{8,12},{12,16},{16,20},{20,24},{24,28},{1,5},{5,9},{9,... | collective-permute-start | bytes 12296 | tf_op jit(solution)/shard_map/ppermute | solution.py:298
  3.7 5.2 %collective-permute-start.1 = (f32[2,512]{1,0:T(2,128)S(1)}, f32[2,512]{1,0:T(2,128)S(1)}, u32[]{:S(2)}, u32[]{:S(2)}) collective-permute-start(f32[2,512]{1,0:T(2,128)S(1)} %get-tuple-element.10), channel_id=1, source_target_pairs={{4,0},{8,4},{12,8},{16,12},{20,16},{24,20},{28,24},{5,1},{9,5},{13... | collective-permute-start | bytes 12296 | tf_op jit(solution)/shard_map/ppermute | solution.py:301
where the time goes:
time: 60.9 us; the launch traced here: 60.4 us
  Pallas kernels  44.7 us (73%)
  local copies, waits for them, and re-layouts  5.67 us (9%)
  starting transfers between devices  3.68 us (6%)
  waiting for transfers between devices  3.15 us (5%)
  between operations  2.35 us (4%)
  other arithmetic  0.78 us (1%)
    pallas_call x1, Pallas kernels, on_device(): pl.pallas_call(functools.partial(gradient_kernel, nb, na, factor), grid=(...  26.9 us
    pallas_call x1, Pallas kernels, on_device(): pl.pallas_call(functools.partial(reduce_kernel, nb, na, n_chan, n_sub, ha...  17.9 us
    unnamed x3, local copies, waits for them, and re-layouts  3.26 us
    ppermute x1, waiting for transfers between devices, on_device(): lax.ppermute(filter_init[:, :harmonics], 'chan', [(i + 1, i) for i in ran...  3.15 us
    ppermute x1, starting transfers between devices, on_device(): lax.ppermute(filter_init[:, owned - harmonics:], 'chan', [(i, i + 1) for...  2.38 us
    broadcast_in_dim x2, local copies, waits for them, and re-layouts, on_device(): jnp.broadcast_to(profile_init.reshape(2, na, LANES)[..., None], (2, na, L...  1.7 us
    ppermute x1, starting transfers between devices, on_device(): lax.ppermute(filter_init[:, :harmonics], 'chan', [(i + 1, i) for i in ran...  1.29 us
  transfers between devices with their start and end apart: 2, of which 1 were waited for; matrix products, arithmetic and copies ran while one was open for 1% of the time, Pallas kernels for 0%

commit v1 on v0

--- a/solution.py
+++ b/solution.py
@@ -38,13 +38,134 @@
     return x
 
 
+def halo_kernel(nb, na, n_chan, f_ref, q_ref, pad_ref, prof_ref, low, high, s_sem, r_sem):
+    chan = lax.axis_index("chan")
+    sub = lax.axis_index("sub")
+    above = lax.rem(chan + 1, n_chan)
+    below = lax.rem(chan + n_chan - 1, n_chan)
+    width = na * LANES
+    owned = nb * LANES
+    barrier = pltpu.get_barrier_semaphore()
+    for c in (above, below):
+        pl.semaphore_signal(barrier, inc=1, device_id=(c, sub), device_id_type=MESH)
+    pl.semaphore_wait(barrier, 2)
+    copies = [
+        pltpu.make_async_remote_copy(
+            src_ref=f_ref.at[:, pl.ds(start, width)], dst_ref=dst, send_sem=s_sem.at[i],
+            recv_sem=r_sem.at[i], device_id=(c, sub), device_id_type=MESH,
+        )
+        for i, (start, dst, c) in enumerate(((owned - width, low, above), (0, high, below)))
+    ]
+    for copy in copies:
+        copy.start()
+    for ri in range(2):
+        for n in range(nb):
+            pad_ref[ri, na + n : na + n + 1] = f_ref[ri : ri + 1, n * LANES : (n + 1) * LANES]
+        for a in range(na):
+            row = q_ref[ri : ri + 1, a * LANES : (a + 1) * LANES]
+            prof_ref[ri, a] = jnp.broadcast_to(row, (LANES, LANES)).T
+    for copy in copies:
+        copy.wait()
+    has_low = chan > 0
+    has_high = chan < n_chan - 1
+    for ri in range(2):
+        for n in range(na):
+            cols = slice(n * LANES, (n + 1) * LANES)
+            pad_ref[ri, n : n + 1] = jnp.where(has_low, low[ri : ri + 1, cols], 0.0)
+            row = na + nb + n
+            pad_ref[ri, row : row + 1] = jnp.where(has_high, high[ri : ri + 1, cols], 0.0)
+
+
 def gradient_kernel(
     nb, na, factor, f_ref, q_ref, x_ref, main_ref, tail_ref, head_ref,
     base_f, base_b, fwd, bwd, up, lo, up_all, lo_all, prof_acc, err_acc,
 ):
     m = pl.program_id(0)
+    last = pl.num_programs(0) - 1
     ext = nb + na
     tile = (8, LANES)
+    pairs = [(ri, g) for ri in range(2) for g in range(2)]
+    lane = lanes_of(tile)
+    zero8 = jnp.zeros(tile, F32)
+
+    def rows(g):
+        return slice(8 * g, 8 * g + 8)
+
+    def shifts(step):
+        right = [lax.rem(16 * step + 8 * g, LANES) for g in range(2)]
+        left = [lax.rem(LANES - t, LANES) for t in right]
+        keep_right = [lane >= t for t in right]
+        keep_left = [lane < LANES - t for t in right]
+        return right, left, keep_right, keep_left
+
+    def build_fwd(step):
+        _, left, _, keep = shifts(step)
+        slot = lax.rem(step, 2)
+        init = tuple(pltpu.roll(base_f[ri, 0], left[g], 1) for ri, g in pairs)
+
+        def one(n, carry):
+            out = []
+            for (ri, g), now in zip(pairs, carry):
+                after = pltpu.roll(base_f[ri, n + 1], left[g], 1)
+                fwd[slot, ri, n, rows(g)] = jnp.where(keep[g], now, after)
+                out.append(after)
+            return tuple(out)
+
+        return init, one, ext - 1
+
+    def build_bwd(step):
+        right, _, keep, _ = shifts(step)
+        slot = lax.rem(step, 2)
+        init = tuple(pltpu.roll(base_b[ri, 0], right[g], 1) for ri, g in pairs)
+
+        def one(n, carry):
+            out = []
+            for (ri, g), before in zip(pairs, carry):
+                now = pltpu.roll(base_b[ri, n + 1], right[g], 1)
+                bwd[slot, ri, n + 1, rows(g)] = jnp.where(keep[g], now, before)
+                out.append(now)
+            return tuple(out)
+
+        return init, one, ext - 1
+
+    def add_shifted(total, parts, shift, pick):
+        def run(step, slot):
+            amount, keep = shift(step)
+            init = (zero8,) * 4
+
+            def one(n, carry):
+                out = []
+                sums = [total[ri, n] for ri in range(2)]
+                for (ri, g), before in zip(pairs, carry):
+                    now = pltpu.roll(parts[slot, ri, n, rows(g)], amount[g], 1)
+                    sums[ri] = sums[ri] + pick(keep[g], now, before)
+                    out.append(now)
+                for ri in range(2):
+                    total[ri, n] = sums[ri]
+                return tuple(out)
+
+            return init, one, ext
+
+        return run
+
+    def right_of(step):
+        right, _, keep, _ = shifts(step)
+        return right, keep
+
+    def left_of(step):
+        _, left, _, keep = shifts(step)
+        return left, keep
+
+    shear_up = add_shifted(up_all, up, right_of, lambda k, now, before: jnp.where(k, now, before))
+    shear_lo = add_shifted(lo_all, lo, left_of, lambda k, now, before: jnp.where(k, before, now))
+
+    def run_all(task):
+        init, one, count = task
+        for n in range(count):
+            init = one(n, init)
+
+    slot = lax.rem(m, 2)
+    other = lax.rem(m + 1, 2)
 
     @pl.when(m == 0)
     def _():
@@ -55,41 +176,33 @@
             base_b[ri] = by_sublane(low, shift_right)
         up_all[...] = jnp.zeros_like(up_all)
         lo_all[...] = jnp.zeros_like(lo_all)
+        up[...] = jnp.zeros_like(up)
+        lo[...] = jnp.zeros_like(lo)
         err_acc[...] = jnp.zeros_like(err_acc)
-
-    lane = lanes_of(tile)
-    for g in range(2):
-        t = 16 * m + 8 * g
-        left = lax.rem(LANES - t, LANES)
-        rows = slice(8 * g, 8 * g + 8)
-        for ri in range(2):
-            now = pltpu.roll(base_f[ri, 0], left, 1)
-            for n in range(ext - 1):
-                after = pltpu.roll(base_f[ri, n + 1], left, 1)
-                fwd[ri, n, rows] = jnp.where(lane < LANES - t, now, after)
-                now = after
-            before = pltpu.roll(base_b[ri, 0], t, 1)
-            for n in range(1, ext):
-                now = pltpu.roll(base_b[ri, n], t, 1)
-                bwd[ri, n, rows] = jnp.where(lane >= t, now, before)
-                before = now
+        run_all(build_fwd(m))
+        run_all(build_bwd(m))
 
     for ri in range(2):
         for n in range(na - 1):
-            up[ri, nb + n] = jnp.zeros((16, LANES), F32)
-            lo[ri, n] = jnp.zeros((16, LANES), F32)
-
+            up[slot, ri, nb + n] = jnp.zeros((16, LANES), F32)
+            lo[slot, ri, n] = jnp.zeros((16, LANES), F32)
+
+    tasks = [
+        build_fwd(m + 1), build_bwd(m + 1), shear_up(m + last, other), shear_lo(m + last, other)
+    ]
     for a in range(na):
         qr = q_ref[0, a]
         qi = q_ref[1, a]
-
-        def body(b, carry, a=a, qr=qr, qi=qi):
-            gr, gi, er = carry
+        init, side, count = tasks[a] if a < 4 else ((), lambda n, carry: carry, 0)
+
+        def body(b, carry, a=a, qr=qr, qi=qi, side=side):
+            gr, gi, er, beside = carry
             cols = pl.ds(pl.multiple_of(b * LANES, LANES), LANES)
             xr = x_ref[0, a, :, cols].astype(F32)
             xi = x_ref[1, a, :, cols].astype(F32)
-            fr, fi = fwd[0, b + a], fwd[1, b + a]
-            br, bi = bwd[0, b - a + na], bwd[1, b - a + na]
+            fr, fi = fwd[slot, 0, b + a], fwd[slot, 1, b + a]
+            br, bi = bwd[slot, 0, b - a + na], bwd[slot, 1, b - a + na]
+            beside = side(b, beside)
             pr = fr * br + fi * bi
             pi = fi * br - fr * bi
             rr = xr - (pr * qr - pi * qi)
@@ -105,43 +218,32 @@
             vi = yr * fi - yi * fr
             iu, il = b + a, b - a + na - 1
             if a == 0:
-                up[0, iu] = ur
-                up[1, iu] = ui
-                lo[0, il] = vr
-                lo[1, il] = vi
+                up[slot, 0, iu] = ur
+                up[slot, 1, iu] = ui
+                lo[slot, 0, il] = vr
+                lo[slot, 1, il] = vi
             else:
-                up[0, iu] = up[0, iu] + ur
-                up[1, iu] = up[1, iu] + ui
-                lo[0, il] = lo[0, il] + vr
-                lo[1, il] = lo[1, il] + vi
-            return gr, gi, er
+                up[slot, 0, iu] = up[slot, 0, iu] + ur
+                up[slot, 1, iu] = up[slot, 1, iu] + ui
+                lo[slot, 0, il] = lo[slot, 0, il] + vr
+                lo[slot, 1, il] = lo[slot, 1, il] + vi
+            return gr, gi, er, beside
 
         zero = jnp.zeros((16, LANES), F32)
-        gr, gi, er = lax.fori_loop(0, nb, body, (zero, zero, zero), unroll=2)
-        rows = pl.ds(pl.multiple_of(16 * m, 16), 16)
-        prof_acc[0, a, rows] = gr
-        prof_acc[1, a, rows] = gi
+        gr, gi, er, beside = lax.fori_loop(0, nb, body, (zero, zero, zero, init), unroll=2)
+        for n in range(nb, count):
+            beside = side(n, beside)
+        group = pl.ds(pl.multiple_of(16 * m, 16), 16)
+        prof_acc[0, a, group] = gr
+        prof_acc[1, a, group] = gi
         err_acc[...] = err_acc[...] + er
-
-    zero8 = jnp.zeros(tile, F32)
-    for g in range(2):
-        t = 16 * m + 8 * g
-        left = lax.rem(LANES - t, LANES)
-        rows = slice(8 * g, 8 * g + 8)
-        for ri in range(2):
-            before = zero8
-            for n in range(ext):
-                now = pltpu.roll(up[ri, n, rows], t, 1) if n < ext - 1 else zero8
-                up_all[ri, n] = up_all[ri, n] + jnp.where(lane >= t, now, before)
-                before = now
-            before = zero8
-            for n in range(ext):
-                now = pltpu.roll(lo[ri, n, rows], left, 1) if n < ext - 1 else zero8
-                lo_all[ri, n] = lo_all[ri, n] + jnp.where(lane < LANES - t, before, now)
-                before = now
-
-    @pl.when(m == pl.num_programs(0) - 1)
+    for task in tasks[na:]:
+        run_all(task)
+
+    @pl.when(m == last)
     def _():
+        run_all(shear_up(m, slot))
+        run_all(shear_lo(m, slot))
         for ri in range(2):
             upper = factor * jnp.sum(by_sublane(up_all[ri], shift_right), axis=1)
             lower = factor * jnp.sum(by_sublane(lo_all[ri], shift_left), axis=1)
@@ -295,19 +397,23 @@
     factor = -2.0 * weight
     main_rows = 2 * nb + 2 * na + 8
 
-    low = lax.ppermute(
-        filter_init[:, owned - harmonics :], "chan", [(i, i + 1) for i in range(n_chan - 1)]
-    )
-    high = lax.ppermute(
-        filter_init[:, :harmonics], "chan", [(i + 1, i) for i in range(n_chan - 1)]
-    )
-    padded = jnp.concatenate([low, filter_init, high], axis=1).reshape(2, nb + 2 * na, LANES)
-    prof = jnp.broadcast_to(
-        profile_init.reshape(2, na, LANES)[..., None], (2, na, LANES, LANES)
-    )
+    whole = pl.BlockSpec(memory_space=pltpu.VMEM)
+    dma = pltpu.SemaphoreType.DMA
+    padded, prof = pl.pallas_call(
+        functools.partial(halo_kernel, nb, na, n_chan),
+        in_specs=[whole] * 2,
+        out_specs=[whole] * 2,
+        out_shape=[
+            jax.ShapeDtypeStruct((2, nb + 2 * na, LANES), F32),
+            jax.ShapeDtypeStruct((2, na, LANES, LANES), F32),
+        ],
+        scratch_shapes=[
+            pltpu.VMEM((2, harmonics), F32), pltpu.VMEM((2, harmonics), F32), dma((2,)), dma((2,)),
+        ],
+        compiler_params=pltpu.CompilerParams(collective_id=1, has_side_effects=True),
+    )(filter_init, profile_init)
     x = spectra.reshape(2, na, LANES, owned)
 
-    whole = pl.BlockSpec(memory_space=pltpu.VMEM)
     main, tail, head = pl.pallas_call(
         functools.partial(gradient_kernel, nb, na, factor),
         grid=(LANES // 16,),
@@ -329,10 +435,10 @@
         scratch_shapes=[
             pltpu.VMEM((2, ext, 8, LANES), F32),
             pltpu.VMEM((2, ext, 8, LANES), F32),
-            pltpu.VMEM((2, ext, 16, LANES), F32),
-            pltpu.VMEM((2, ext, 16, LANES), F32),
-            pltpu.VMEM((2, ext, 16, LANES), F32),
-            pltpu.VMEM((2, ext, 16, LANES), F32),
+            pltpu.VMEM((2, 2, ext, 16, LANES), F32),
+            pltpu.VMEM((2, 2, ext, 16, LANES), F32),
+            pltpu.VMEM((2, 2, ext, 16, LANES), F32),
+            pltpu.VMEM((2, 2, ext, 16, LANES), F32),
             pltpu.VMEM((2, ext, 8, LANES), F32),
             pltpu.VMEM((2, ext, 8, LANES), F32),
             pltpu.VMEM((2, na, LANES, LANES), F32),
@@ -340,7 +446,6 @@
         ],
     )(padded, prof, x)
 
-    dma = pltpu.SemaphoreType.DMA
     return pl.pallas_call(
         functools.partial(reduce_kernel, nb, na, n_chan, n_sub, harmonics, weight),
         in_specs=[whole] * 5,

time: 60.9 us -> 87.7 us (1.44)
  Pallas kernels: 44.7 us -> 82.3 us
  starting transfers between devices: 3.68 us -> 0 us
  waiting for transfers between devices: 3.15 us -> 0 us
  local copies, waits for them, and re-layouts: 5.67 us -> 2.65 us
    pallas_call x1, Pallas kernels: 26.9 us -> 59.5 us  [on_device(): pl.pallas_call(functools.partial(gradient_kernel, nb, na, factor), grid=(...]
    pallas_call x0 -> x1, Pallas kernels: none -> 6.96 us  [on_device(): pl.pallas_call(functools.partial(halo_kernel, nb, na, n_chan), in_specs=[...]
    ppermute x2 -> x0, starting transfers between devices: 3.68 us -> none  [the longest x1 2.38 us: on_device(): lax.ppermute(filter_init[:, owned - harmonics:], 'chan', [(i, i + 1) for...]
    ppermute x2 -> x0, waiting for transfers between devices: 3.15 us -> none  [the longest x1 3.15 us: on_device(): lax.ppermute(filter_init[:, :harmonics], 'chan', [(i + 1, i) for i in ran...]
    pallas_call x1, Pallas kernels: 17.9 us -> 15.9 us  [on_device(): pl.pallas_call(functools.partial(reduce_kernel, nb, na, n_chan, n_sub, ha...]
    broadcast_in_dim x2 -> x0, local copies, waits for them, and re-layouts: 1.7 us -> none  [on_device(): jnp.broadcast_to(profile_init.reshape(2, na, LANES)[..., None], (2, na, L...]
    unnamed x3 -> x2, local copies, waits for them, and re-layouts: 3.26 us -> 2.65 us
  transfers between devices with their start and end apart: 2 -> 0, of which waited for: 1 -> 0; matrix products, arithmetic and copies ran while one was open for 1% -> 0% of each run, Pallas kernels for 0% -> 0%
where the time goes in v1:
time: 87.7 us; the launch traced here: 87.3 us
  Pallas kernels  82.3 us (94%)
  local copies, waits for them, and re-layouts  2.65 us (3%)
  between operations  2.34 us (3%)
    pallas_call x1, Pallas kernels, on_device(): pl.pallas_call(functools.partial(gradient_kernel, nb, na, factor), grid=(...  59.5 us
    pallas_call x1, Pallas kernels, on_device(): pl.pallas_call(functools.partial(reduce_kernel, nb, na, n_chan, n_sub, ha...  15.9 us
    pallas_call x1, Pallas kernels, on_device(): pl.pallas_call(functools.partial(halo_kernel, nb, na, n_chan), in_specs=[...  6.96 us
    unnamed x2, local copies, waits for them, and re-layouts  2.65 us

profile of v1, /device:TPU:0, one launch (start us, length us, event | category | flops | bytes accessed | tf_op | source)
XLA Modules:
  0.0 87.3 jit_solution(7693022193369182898)
XLA Ops:
  0.6 7.0 %shard_map.58 = (f32[2,40,128]{2,1,0:T(8,128)}, f32[2,4,128,128]{3,2,1,0:T(8,128)}) custom-call(f32[2,4096]{1,0:T(2,128)} %f_ref.3, f32[2,512]{1,0:T(2,128)} %q_ref.3), custom_call_target="tpu_custom_call" | custom-call | tf_op jit(solution)/shard_map/pallas_call | solution.py:402
  7.6 59.5 %shard_map.59 = (f32[80,128]{1,0:T(8,128)}, f32[8,128]{1,0:T(8,128)}, f32[8,128]{1,0:T(8,128)}) custom-call(f32[2,40,128]{2,1,0:T(8,128)} %get-tuple-element.8.f_ref, f32[2,4,128,128]{3,2,1,0:T(8,128)} %get-tuple-element.9.q_ref, bf16[2,4,128,4096]{3,2,1,0:T(8,128)(2,1)} %bitcast.1), custom_call_target="tpu_custom_call" | custom-call | tf_op jit(solution)/shard_map/pallas_call | solution.py:417
  67.1 15.9 %shard_map.60 = (f32[2,4096]{1,0:T(2,128)}, f32[2,512]{1,0:T(2,128)}, f32[1]{0:T(128)}) custom-call(f32[2,4096]{1,0:T(2,128)} %f_ref.3, f32[2,512]{1,0:T(2,128)} %q_ref.3, f32[80,128]{1,0:T(8,128)} %get-tuple-element.10.main_ref, f32[8,128]{1,0:T(8,128)} %get-tuple-element.11.tail_ref, f32[8,128]{1,0:T(8,128)} %get-tuple-element.12.head_ref), custom_call_target="tpu_custom_call" | custom-call | tf_op jit(solution)/shard_map/pallas_call | solution.py:449
  83.0 1.4 %copy.9 = f32[2,4096]{1,0:T(2,128)} copy(f32[2,4096]{1,0:T(2,128)} %get-tuple-element.16) | data formatting | bytes 65536
  84.3 1.3 %copy.10 = f32[2,512]{1,0:T(2,128)} copy(f32[2,512]{1,0:T(2,128)} %get-tuple-element.17) | data formatting | bytes 8192

commit v2 on v1

--- a/solution.py
+++ b/solution.py
@@ -78,10 +78,13 @@
 
 def gradient_kernel(
     nb, na, factor, f_ref, q_ref, x_ref, main_ref, tail_ref, head_ref,
-    base_f, base_b, fwd, bwd, up, lo, up_all, lo_all, prof_acc, err_acc,
+    base_f, base_b, fwd0, bwd0, up0, lo0, fwd1, bwd1, up1, lo1,
+    up_all, lo_all, prof_acc, err_acc,
 ):
-    m = pl.program_id(0)
-    last = pl.num_programs(0) - 1
+    pair = pl.program_id(0)
+    last_pair = pl.num_programs(0) - 1
+    last = 2 * pl.num_programs(0) - 1
+    sets = ((fwd0, bwd0, up0, lo0), (fwd1, bwd1, up1, lo1))
     ext = nb + na
     tile = (8, LANES)
     pairs = [(ri, g) for ri in range(2) for g in range(2)]
@@ -98,38 +101,36 @@
         keep_left = [lane < LANES - t for t in right]
         return right, left, keep_right, keep_left
 
-    def build_fwd(step):
+    def build_fwd(step, fwd):
         _, left, _, keep = shifts(step)
-        slot = lax.rem(step, 2)
         init = tuple(pltpu.roll(base_f[ri, 0], left[g], 1) for ri, g in pairs)
 
         def one(n, carry):
             out = []
             for (ri, g), now in zip(pairs, carry):
                 after = pltpu.roll(base_f[ri, n + 1], left[g], 1)
-                fwd[slot, ri, n, rows(g)] = jnp.where(keep[g], now, after)
+                fwd[ri, n, rows(g)] = jnp.where(keep[g], now, after)
                 out.append(after)
             return tuple(out)
 
         return init, one, ext - 1
 
-    def build_bwd(step):
+    def build_bwd(step, bwd):
         right, _, keep, _ = shifts(step)
-        slot = lax.rem(step, 2)
         init = tuple(pltpu.roll(base_b[ri, 0], right[g], 1) for ri, g in pairs)
 
         def one(n, carry):
             out = []
             for (ri, g), before in zip(pairs, carry):
                 now = pltpu.roll(base_b[ri, n + 1], right[g], 1)
-                bwd[slot, ri, n + 1, rows(g)] = jnp.where(keep[g], now, before)
+                bwd[ri, n + 1, rows(g)] = jnp.where(keep[g], now, before)
                 out.append(now)
             return tuple(out)
 
         return init, one, ext - 1
 
-    def add_shifted(total, parts, shift, pick):
-        def run(step, slot):
+    def add_shifted(total, shift, pick):
+        def run(step, parts):
             amount, keep = shift(step)
             init = (zero8,) * 4
 
@@ -137,7 +138,7 @@
                 out = []
                 sums = [total[ri, n] for ri in range(2)]
                 for (ri, g), before in zip(pairs, carry):
-                    now = pltpu.roll(parts[slot, ri, n, rows(g)], amount[g], 1)
+                    now = pltpu.roll(parts[ri, n, rows(g)], amount[g], 1)
                     sums[ri] = sums[ri] + pick(keep[g], now, before)
                     out.append(now)
                 for ri in range(2):
@@ -156,18 +157,15 @@
         _, left, _, keep = shifts(step)
         return left, keep
 
-    shear_up = add_shifted(up_all, up, right_of, lambda k, now, before: jnp.where(k, now, before))
-    shear_lo = add_shifted(lo_all, lo, left_of, lambda k, now, before: jnp.where(k, before, now))
+    shear_up = add_shifted(up_all, right_of, lambda k, now, before: jnp.where(k, now, before))
+    shear_lo = add_shifted(lo_all, left_of, lambda k, now, before: jnp.where(k, before, now))
 
     def run_all(task):
         init, one, count = task
         for n in range(count):
             init = one(n, init)
 
-    slot = lax.rem(m, 2)
-    other = lax.rem(m + 1, 2)
-
-    @pl.when(m == 0)
+    @pl.when(pair == 0)
     def _():
         for ri in range(2):
             high = jnp.broadcast_to(f_ref[ri, na:, :][:, None, :], (ext, 8, LANES))
@@ -176,74 +174,81 @@
             base_b[ri] = by_sublane(low, shift_right)
         up_all[...] = jnp.zeros_like(up_all)
         lo_all[...] = jnp.zeros_like(lo_all)
-        up[...] = jnp.zeros_like(up)
-        lo[...] = jnp.zeros_like(lo)
+        for _, _, up, lo in sets:
+            up[...] = jnp.zeros_like(up)
+            lo[...] = jnp.zeros_like(lo)
         err_acc[...] = jnp.zeros_like(err_acc)
-        run_all(build_fwd(m))
-        run_all(build_bwd(m))
-
-    for ri in range(2):
-        for n in range(na - 1):
-            up[slot, ri, nb + n] = jnp.zeros((16, LANES), F32)
-            lo[slot, ri, n] = jnp.zeros((16, LANES), F32)
-
-    tasks = [
-        build_fwd(m + 1), build_bwd(m + 1), shear_up(m + last, other), shear_lo(m + last, other)
-    ]
-    for a in range(na):
-        qr = q_ref[0, a]
-        qi = q_ref[1, a]
-        init, side, count = tasks[a] if a < 4 else ((), lambda n, carry: carry, 0)
-
-        def body(b, carry, a=a, qr=qr, qi=qi, side=side):
-            gr, gi, er, beside = carry
-            cols = pl.ds(pl.multiple_of(b * LANES, LANES), LANES)
-            xr = x_ref[0, a, :, cols].astype(F32)
-            xi = x_ref[1, a, :, cols].astype(F32)
-            fr, fi = fwd[slot, 0, b + a], fwd[slot, 1, b + a]
-            br, bi = bwd[slot, 0, b - a + na], bwd[slot, 1, b - a + na]
-            beside = side(b, beside)
-            pr = fr * br + fi * bi
-            pi = fi * br - fr * bi
-            rr = xr - (pr * qr - pi * qi)
-            ri = xi - (pr * qi + pi * qr)
-            er = er + (rr * rr + ri * ri)
-            gr = gr + (rr * pr + ri * pi)
-            gi = gi + (ri * pr - rr * pi)
-            yr = rr * qr + ri * qi
-            yi = ri * qr - rr * qi
-            ur = yr * br - yi * bi
-            ui = yr * bi + yi * br
-            vr = yr * fr + yi * fi
-            vi = yr * fi - yi * fr
-            iu, il = b + a, b - a + na - 1
-            if a == 0:
-                up[slot, 0, iu] = ur
-                up[slot, 1, iu] = ui
-                lo[slot, 0, il] = vr
-                lo[slot, 1, il] = vi
-            else:
-                up[slot, 0, iu] = up[slot, 0, iu] + ur
-                up[slot, 1, iu] = up[slot, 1, iu] + ui
-                lo[slot, 0, il] = lo[slot, 0, il] + vr
-                lo[slot, 1, il] = lo[slot, 1, il] + vi
-            return gr, gi, er, beside
-
-        zero = jnp.zeros((16, LANES), F32)
-        gr, gi, er, beside = lax.fori_loop(0, nb, body, (zero, zero, zero, init), unroll=2)
-        for n in range(nb, count):
-            beside = side(n, beside)
-        group = pl.ds(pl.multiple_of(16 * m, 16), 16)
-        prof_acc[0, a, group] = gr
-        prof_acc[1, a, group] = gi
-        err_acc[...] = err_acc[...] + er
-    for task in tasks[na:]:
-        run_all(task)
-
-    @pl.when(m == last)
+        run_all(build_fwd(0 * pair, fwd0))
+        run_all(build_bwd(0 * pair, bwd0))
+
+    for half in range(2):
+        m = 2 * pair + half
+        held = slice(16 * half, 16 * half + 16)
+        fwd, bwd, up, lo = sets[half]
+        next_fwd, next_bwd, prev_up, prev_lo = sets[1 - half]
+        for ri in range(2):
+            for n in range(na - 1):
+                up[ri, nb + n] = jnp.zeros((16, LANES), F32)
+                lo[ri, n] = jnp.zeros((16, LANES), F32)
+
+        tasks = [
+            build_fwd(m + 1, next_fwd), build_bwd(m + 1, next_bwd),
+            shear_up(m + last, prev_up), shear_lo(m + last, prev_lo),
+        ]
+        for a in range(na):
+            qr = q_ref[0, a, held]
+            qi = q_ref[1, a, held]
+            init, side, count = tasks[a] if a < 4 else ((), lambda n, carry: carry, 0)
+
+            def body(b, carry, a=a, qr=qr, qi=qi, side=side):
+                gr, gi, er, beside = carry
+                cols = pl.ds(pl.multiple_of(b * LANES, LANES), LANES)
+                xr = x_ref[0, a, held, cols].astype(F32)
+                xi = x_ref[1, a, held, cols].astype(F32)
+                fr, fi = fwd[0, b + a], fwd[1, b + a]
+                br, bi = bwd[0, b - a + na], bwd[1, b - a + na]
+                beside = side(b, beside)
+                pr = fr * br + fi * bi
+                pi = fi * br - fr * bi
+                rr = xr - (pr * qr - pi * qi)
+                ri = xi - (pr * qi + pi * qr)
+                er = er + (rr * rr + ri * ri)
+                gr = gr + (rr * pr + ri * pi)
+                gi = gi + (ri * pr - rr * pi)
+                yr = rr * qr + ri * qi
+                yi = ri * qr - rr * qi
+                ur = yr * br - yi * bi
+                ui = yr * bi + yi * br
+                vr = yr * fr + yi * fi
+                vi = yr * fi - yi * fr
+                iu, il = b + a, b - a + na - 1
+                if a == 0:
+                    up[0, iu] = ur
+                    up[1, iu] = ui
+                    lo[0, il] = vr
+                    lo[1, il] = vi
+                else:
+                    up[0, iu] = up[0, iu] + ur
+                    up[1, iu] = up[1, iu] + ui
+                    lo[0, il] = lo[0, il] + vr
+                    lo[1, il] = lo[1, il] + vi
+                return gr, gi, er, beside
+
+            zero = jnp.zeros((16, LANES), F32)
+            gr, gi, er, beside = lax.fori_loop(0, nb, body, (zero, zero, zero, init), unroll=4)
+            for n in range(nb, count):
+                beside = side(n, beside)
+            group = pl.ds(pl.multiple_of(16 * m, 16), 16)
+            prof_acc[0, a, group] = gr
+            prof_acc[1, a, group] = gi
+            err_acc[...] = err_acc[...] + er
+        for task in tasks[na:]:
+            run_all(task)
+
+    @pl.when(pair == last_pair)
     def _():
-        run_all(shear_up(m, slot))
-        run_all(shear_lo(m, slot))
+        run_all(shear_up(2 * pair + 1, up1))
+        run_all(shear_lo(2 * pair + 1, lo1))
         for ri in range(2):
             upper = factor * jnp.sum(by_sublane(up_all[ri], shift_right), axis=1)
             lower = factor * jnp.sum(by_sublane(lo_all[ri], shift_left), axis=1)
@@ -263,7 +268,7 @@
 
 
 def reduce_kernel(
-    nb, na, n_chan, n_sub, harmonics, weight, f_ref, q_ref, main_ref, tail_ref, head_ref,
+    nb, na, n_chan, n_sub, harmonics, weight, main_ref, tail_ref, head_ref,
     out_ref, prof_ref, misfit_ref,
     mains, tails, heads, packs, pack,
     s_main, r_main, s_tail, r_tail, s_head, r_head, s_pack, r_pack,
@@ -373,14 +378,14 @@
         step = grads[ri] * scale
         for n in range(nb):
             cols = slice(n * LANES, (n + 1) * LANES)
-            out_ref[ri : ri + 1, cols] = f_ref[ri : ri + 1, cols] - step[n : n + 1]
+            out_ref[ri : ri + 1, cols] = step[n : n + 1]
     mean = jnp.sum(prof_grad * prof_grad, keepdims=True) / (2 * harmonics)
     prof_step = prof_grad * (profile_rate / jnp.sqrt(mean + epsilon))
     for ri in range(2):
         for a in range(na):
             cols = slice(a * LANES, (a + 1) * LANES)
             row = ri * na + a
-            prof_ref[ri : ri + 1, cols] = q_ref[ri : ri + 1, cols] - prof_step[row : row + 1]
+            prof_ref[ri : ri + 1, cols] = prof_step[row : row + 1]
     for copy in exchanges:
         copy.wait_send()
 
@@ -416,11 +421,11 @@
 
     main, tail, head = pl.pallas_call(
         functools.partial(gradient_kernel, nb, na, factor),
-        grid=(LANES // 16,),
+        grid=(LANES // 32,),
         in_specs=[
             pl.BlockSpec((2, nb + 2 * na, LANES), lambda m: (0, 0, 0)),
-            pl.BlockSpec((2, na, 16, LANES), lambda m: (0, 0, m, 0)),
-            pl.BlockSpec((2, na, 16, owned), lambda m: (0, 0, m, 0)),
+            pl.BlockSpec((2, na, 32, LANES), lambda m: (0, 0, m, 0)),
+            pl.BlockSpec((2, na, 32, owned), lambda m: (0, 0, m, 0)),
         ],
         out_specs=[
             pl.BlockSpec((main_rows, LANES), lambda m: (0, 0)),
@@ -435,10 +440,14 @@
         scratch_shapes=[
             pltpu.VMEM((2, ext, 8, LANES), F32),
             pltpu.VMEM((2, ext, 8, LANES), F32),
-            pltpu.VMEM((2, 2, ext, 16, LANES), F32),
-            pltpu.VMEM((2, 2, ext, 16, LANES), F32),
-            pltpu.VMEM((2, 2, ext, 16, LANES), F32),
-            pltpu.VMEM((2, 2, ext, 16, LANES), F32),
+            pltpu.VMEM((2, ext, 16, LANES), F32),
+            pltpu.VMEM((2, ext, 16, LANES), F32),
+            pltpu.VMEM((2, ext, 16, LANES), F32),
+            pltpu.VMEM((2, ext, 16, LANES), F32),
+            pltpu.VMEM((2, ext, 16, LANES), F32),
+            pltpu.VMEM((2, ext, 16, LANES), F32),
+            pltpu.VMEM((2, ext, 16, LANES), F32),
+            pltpu.VMEM((2, ext, 16, LANES), F32),
             pltpu.VMEM((2, ext, 8, LANES), F32),
             pltpu.VMEM((2, ext, 8, LANES), F32),
             pltpu.VMEM((2, na, LANES, LANES), F32),
@@ -446,9 +455,9 @@
         ],
     )(padded, prof, x)
 
-    return pl.pallas_call(
+    step, prof_step, misfit = pl.pallas_call(
         functools.partial(reduce_kernel, nb, na, n_chan, n_sub, harmonics, weight),
-        in_specs=[whole] * 5,
+        in_specs=[whole] * 3,
         out_specs=[whole, whole, pl.BlockSpec(memory_space=pltpu.SMEM)],
         out_shape=[
             jax.ShapeDtypeStruct((2, owned), F32),
@@ -467,7 +476,8 @@
             dma((n_chan,)), dma((n_chan,)),
         ],
         compiler_params=pltpu.CompilerParams(collective_id=0, has_side_effects=True),
-    )(filter_init, profile_init, main, tail, head)
+    )(main, tail, head)
+    return (filter_init - step, profile_init - prof_step, misfit)
 
 
 def solution(mesh):

time: 87.7 us -> 59 us (0.67)
  Pallas kernels: 82.3 us -> 53.6 us
  other arithmetic: 0 us -> 2.67 us
  local copies, waits for them, and re-layouts: 2.65 us -> 0.01 us
    pallas_call x1, Pallas kernels: 59.5 us -> 30.8 us  [on_device(): pl.pallas_call(functools.partial(gradient_kernel, nb, na, factor), grid=(...]
    sub x0 -> x2, other arithmetic: none -> 2.67 us  [on_device(): return (filter_init - step, profile_init - prof_step, misfit)]
    unnamed x2 -> x4, local copies, waits for them, and re-layouts: 2.65 us -> 0.01 us
where the time goes in v2:
time: 59 us; the launch traced here: 58.7 us
  Pallas kernels  53.6 us (91%)
  other arithmetic  2.67 us (5%)
  between operations  2.36 us (4%)
    pallas_call x1, Pallas kernels, on_device(): pl.pallas_call(functools.partial(gradient_kernel, nb, na, factor), grid=(...  30.8 us
    pallas_call x1, Pallas kernels, on_device(): pl.pallas_call(functools.partial(reduce_kernel, nb, na, n_chan, n_sub, ha...  15.8 us
    pallas_call x1, Pallas kernels, on_device(): pl.pallas_call(functools.partial(halo_kernel, nb, na, n_chan), in_specs=[...  7.01 us
    sub x2, other arithmetic, on_device(): return (filter_init - step, profile_init - prof_step, misfit)  2.67 us

profile of v2, /device:TPU:0, one launch (start us, length us, event | category | flops | bytes accessed | tf_op | source)
XLA Modules:
  0.0 58.7 jit_solution(10802282841661471575)
XLA Ops:
  0.6 0.0 copy-start.1
  0.6 0.0 copy-start
  0.6 7.0 %shard_map.58 = (f32[2,40,128]{2,1,0:T(8,128)}, f32[2,4,128,128]{3,2,1,0:T(8,128)}) custom-call(f32[2,4096]{1,0:T(2,128)} %f_ref.1, f32[2,512]{1,0:T(2,128)} %q_ref.1), custom_call_target="tpu_custom_call" | custom-call | tf_op jit(solution)/shard_map/pallas_call | solution.py:407
  7.7 30.8 %shard_map.59 = (f32[80,128]{1,0:T(8,128)}, f32[8,128]{1,0:T(8,128)}, f32[8,128]{1,0:T(8,128)}) custom-call(f32[2,40,128]{2,1,0:T(8,128)} %get-tuple-element.11.f_ref, f32[2,4,128,128]{3,2,1,0:T(8,128)} %get-tuple-element.12.q_ref, bf16[2,4,128,4096]{3,2,1,0:T(8,128)(2,1)} %bitcast.1), custom_call_target="tpu_custom_call" | custom-call | tf_op jit(solution)/shard_map/pallas_call | solution.py:422
  38.5 15.8 %shard_map.60 = (f32[2,4096]{1,0:T(2,128)}, f32[2,512]{1,0:T(2,128)}, f32[1]{0:T(128)}) custom-call(f32[80,128]{1,0:T(8,128)} %get-tuple-element.13.main_ref, f32[8,128]{1,0:T(8,128)} %get-tuple-element.14.tail_ref, f32[8,128]{1,0:T(8,128)} %get-tuple-element.15.head_ref), custom_call_target="tpu_custom_call" | custom-call | tf_op jit(solution)/shard_map/pallas_call | solution.py:458
  54.3 0.0 copy-done
  54.3 1.4 %sub.6 = f32[2,4096]{1,0:T(2,128)} subtract(f32[2,4096]{1,0:T(2,128)S(1)} %copy-done, f32[2,4096]{1,0:T(2,128)} %get-tuple-element.16) | non-fusion elementwise | flops 8192 | bytes 98304 | tf_op jit(solution)/shard_map/sub | solution.py:480
  55.7 0.0 copy-done.1
  55.7 1.3 %sub.7 = f32[2,512]{1,0:T(2,128)} subtract(f32[2,512]{1,0:T(2,128)S(1)} %copy-done.1, f32[2,512]{1,0:T(2,128)} %get-tuple-element.17) | non-fusion elementwise | flops 1024 | bytes 12288 | tf_op jit(solution)/shard_map/sub | solution.py:480
Async XLA Ops:
  0.6 55.1 %copy-start.1 = (f32[2,512]{1,0:T(2,128)S(1)}, f32[2,512]{1,0:T(2,128)}, u32[]{:S(2)}) copy-start(f32[2,512]{1,0:T(2,128)} %q_ref.1) | copy-start | bytes 12292
  0.6 53.7 %copy-start = (f32[2,4096]{1,0:T(2,128)S(1)}, f32[2,4096]{1,0:T(2,128)}, u32[]{:S(2)}) copy-start(f32[2,4096]{1,0:T(2,128)} %f_ref.1) | copy-start | bytes 98308

commit v3 on v2

--- a/solution.py
+++ b/solution.py
@@ -235,7 +235,7 @@
                 return gr, gi, er, beside
 
             zero = jnp.zeros((16, LANES), F32)
-            gr, gi, er, beside = lax.fori_loop(0, nb, body, (zero, zero, zero, init), unroll=4)
+            gr, gi, er, beside = lax.fori_loop(0, nb, body, (zero, zero, zero, init), unroll=nb)
             for n in range(nb, count):
                 beside = side(n, beside)
             group = pl.ds(pl.multiple_of(16 * m, 16), 16)

time: 59 us -> 49.6 us (0.84)
  Pallas kernels: 53.6 us -> 44.2 us
    pallas_call x1, Pallas kernels: 30.8 us -> 21.4 us  [on_device(): pl.pallas_call(functools.partial(gradient_kernel, nb, na, factor), grid=(...]
where the time goes in v3:
time: 49.6 us; the launch traced here: 49.3 us
  Pallas kernels  44.2 us (89%)
  other arithmetic  2.67 us (5%)
  between operations  2.36 us (5%)
    pallas_call x1, Pallas kernels, on_device(): pl.pallas_call(functools.partial(gradient_kernel, nb, na, factor), grid=(...  21.4 us
    pallas_call x1, Pallas kernels, on_device(): pl.pallas_call(functools.partial(reduce_kernel, nb, na, n_chan, n_sub, ha...  15.8 us
    pallas_call x1, Pallas kernels, on_device(): pl.pallas_call(functools.partial(halo_kernel, nb, na, n_chan), in_specs=[...  7.01 us
    sub x2, other arithmetic, on_device(): return (filter_init - step, profile_init - prof_step, misfit)  2.67 us

profile of v3, /device:TPU:0, one launch (start us, length us, event | category | flops | bytes accessed | tf_op | source)
XLA Modules:
  0.0 49.3 jit_solution(5317826727643337532)
XLA Ops:
  0.6 0.0 copy-start.1
  0.6 0.0 copy-start
  0.6 7.0 %shard_map.58 = (f32[2,40,128]{2,1,0:T(8,128)}, f32[2,4,128,128]{3,2,1,0:T(8,128)}) custom-call(f32[2,4096]{1,0:T(2,128)} %f_ref.1, f32[2,512]{1,0:T(2,128)} %q_ref.1), custom_call_target="tpu_custom_call" | custom-call | tf_op jit(solution)/shard_map/pallas_call | solution.py:407
  7.7 21.4 %shard_map.59 = (f32[80,128]{1,0:T(8,128)}, f32[8,128]{1,0:T(8,128)}, f32[8,128]{1,0:T(8,128)}) custom-call(f32[2,40,128]{2,1,0:T(8,128)} %get-tuple-element.11.f_ref, f32[2,4,128,128]{3,2,1,0:T(8,128)} %get-tuple-element.12.q_ref, bf16[2,4,128,4096]{3,2,1,0:T(8,128)(2,1)} %bitcast.1), custom_call_target="tpu_custom_call" | custom-call | tf_op jit(solution)/shard_map/pallas_call | solution.py:422
  29.1 15.8 %shard_map.60 = (f32[2,4096]{1,0:T(2,128)}, f32[2,512]{1,0:T(2,128)}, f32[1]{0:T(128)}) custom-call(f32[80,128]{1,0:T(8,128)} %get-tuple-element.13.main_ref, f32[8,128]{1,0:T(8,128)} %get-tuple-element.14.tail_ref, f32[8,128]{1,0:T(8,128)} %get-tuple-element.15.head_ref), custom_call_target="tpu_custom_call" | custom-call | tf_op jit(solution)/shard_map/pallas_call | solution.py:458
  44.9 0.0 copy-done
  44.9 1.4 %sub.6 = f32[2,4096]{1,0:T(2,128)} subtract(f32[2,4096]{1,0:T(2,128)S(1)} %copy-done, f32[2,4096]{1,0:T(2,128)} %get-tuple-element.16) | non-fusion elementwise | flops 8192 | bytes 98304 | tf_op jit(solution)/shard_map/sub | solution.py:480
  46.3 0.0 copy-done.1
  46.3 1.3 %sub.7 = f32[2,512]{1,0:T(2,128)} subtract(f32[2,512]{1,0:T(2,128)S(1)} %copy-done.1, f32[2,512]{1,0:T(2,128)} %get-tuple-element.17) | non-fusion elementwise | flops 1024 | bytes 12288 | tf_op jit(solution)/shard_map/sub | solution.py:480
Async XLA Ops:
  0.6 45.7 %copy-start.1 = (f32[2,512]{1,0:T(2,128)S(1)}, f32[2,512]{1,0:T(2,128)}, u32[]{:S(2)}) copy-start(f32[2,512]{1,0:T(2,128)} %q_ref.1) | copy-start | bytes 12292
  0.6 44.2 %copy-start = (f32[2,4096]{1,0:T(2,128)S(1)}, f32[2,4096]{1,0:T(2,128)}, u32[]{:S(2)}) copy-start(f32[2,4096]{1,0:T(2,128)} %f_ref.1) | copy-start | bytes 98308

commit v4 on v3

--- a/solution.py
+++ b/solution.py
@@ -38,7 +38,7 @@
     return x
 
 
-def halo_kernel(nb, na, n_chan, f_ref, q_ref, pad_ref, prof_ref, low, high, s_sem, r_sem):
+def halo_part(nb, na, n_chan, n_sub, f_ref, q_ref, pad_ref, prof_ref, low, high, s_sem, r_sem):
     chan = lax.axis_index("chan")
     sub = lax.axis_index("sub")
     above = lax.rem(chan + 1, n_chan)
@@ -46,24 +46,33 @@
     width = na * LANES
     owned = nb * LANES
     barrier = pltpu.get_barrier_semaphore()
-    for c in (above, below):
-        pl.semaphore_signal(barrier, inc=1, device_id=(c, sub), device_id_type=MESH)
-    pl.semaphore_wait(barrier, 2)
-    copies = [
-        pltpu.make_async_remote_copy(
-            src_ref=f_ref.at[:, pl.ds(start, width)], dst_ref=dst, send_sem=s_sem.at[i],
-            recv_sem=r_sem.at[i], device_id=(c, sub), device_id_type=MESH,
-        )
-        for i, (start, dst, c) in enumerate(((owned - width, low, above), (0, high, below)))
-    ]
-    for copy in copies:
-        copy.start()
+    greeted = 0
+    for off in range(n_sub):
+        peer = lax.rem(sub + off, n_sub)
+        for c in (above, below) + ((chan,) if off else ()):
+            pl.semaphore_signal(barrier, inc=1, device_id=(c, peer), device_id_type=MESH)
+            greeted += 1
+    for off in range(2, n_chan - 1):
+        pl.semaphore_signal(
+            barrier, inc=1, device_id=(lax.rem(chan + off, n_chan), sub), device_id_type=MESH
+        )
+        greeted += 1
     for ri in range(2):
         for n in range(nb):
             pad_ref[ri, na + n : na + n + 1] = f_ref[ri : ri + 1, n * LANES : (n + 1) * LANES]
         for a in range(na):
             row = q_ref[ri : ri + 1, a * LANES : (a + 1) * LANES]
             prof_ref[ri, a] = jnp.broadcast_to(row, (LANES, LANES)).T
+    pl.semaphore_wait(barrier, greeted)
+    copies = [
+        pltpu.make_async_remote_copy(
+            src_ref=f_ref.at[:, pl.ds(start, width)], dst_ref=dst, send_sem=s_sem.at[i],
+            recv_sem=r_sem.at[i], device_id=(c, sub), device_id_type=MESH,
+        )
+        for i, (start, dst, c) in enumerate(((owned - width, low, above), (0, high, below)))
+    ]
+    for copy in copies:
+        copy.start()
     for copy in copies:
         copy.wait()
     has_low = chan > 0
@@ -77,7 +86,9 @@
 
 
 def gradient_kernel(
-    nb, na, factor, f_ref, q_ref, x_ref, main_ref, tail_ref, head_ref,
+    nb, na, n_chan, n_sub, harmonics, weight, factor, filter_ref, profile_ref, x_ref,
+    out_ref, prof_ref, misfit_ref,
+    f_ref, q_ref, halo_low, halo_high, s_halo, r_halo, main_ref, tail_ref, head_ref, reduce_refs,
     base_f, base_b, fwd0, bwd0, up0, lo0, fwd1, bwd1, up1, lo1,
     up_all, lo_all, prof_acc, err_acc,
 ):
@@ -167,6 +178,10 @@
 
     @pl.when(pair == 0)
     def _():
+        halo_part(
+            nb, na, n_chan, n_sub, filter_ref, profile_ref, f_ref, q_ref,
+            halo_low, halo_high, s_halo, r_halo,
+        )
         for ri in range(2):
             high = jnp.broadcast_to(f_ref[ri, na:, :][:, None, :], (ext, 8, LANES))
             base_f[ri] = by_sublane(high, shift_left)
@@ -184,6 +199,7 @@
     for half in range(2):
         m = 2 * pair + half
         held = slice(16 * half, 16 * half + 16)
+        held_q = pl.ds(pl.multiple_of(16 * m, 16), 16)
         fwd, bwd, up, lo = sets[half]
         next_fwd, next_bwd, prev_up, prev_lo = sets[1 - half]
         for ri in range(2):
@@ -196,8 +212,8 @@
             shear_up(m + last, prev_up), shear_lo(m + last, prev_lo),
         ]
         for a in range(na):
-            qr = q_ref[0, a, held]
-            qi = q_ref[1, a, held]
+            qr = q_ref[0, a, held_q]
+            qi = q_ref[1, a, held_q]
             init, side, count = tasks[a] if a < 4 else ((), lambda n, carry: carry, 0)
 
             def body(b, carry, a=a, qr=qr, qi=qi, side=side):
@@ -262,12 +278,16 @@
                 )
                 row = 2 * nb + ri * na + a
                 main_ref[row : row + 1] = factor * sums[:1]
-        main_ref[2 * nb + 2 * na : 2 * nb + 2 * na + 1] = jnp.sum(
-            err_acc[...], axis=0, keepdims=True
-        )
-
-
-def reduce_kernel(
+        main_ref[2 * nb + 2 * na :] = jnp.broadcast_to(
+            jnp.sum(err_acc[...], axis=0, keepdims=True), tile
+        )
+        reduce_part(
+            nb, na, n_chan, n_sub, harmonics, weight, main_ref, tail_ref, head_ref,
+            out_ref, prof_ref, misfit_ref, *reduce_refs,
+        )
+
+
+def reduce_part(
     nb, na, n_chan, n_sub, harmonics, weight, main_ref, tail_ref, head_ref,
     out_ref, prof_ref, misfit_ref,
     mains, tails, heads, packs, pack,
@@ -277,20 +297,6 @@
     sub = lax.axis_index("sub")
     above = lax.rem(chan + 1, n_chan)
     below = lax.rem(chan + n_chan - 1, n_chan)
-
-    barrier = pltpu.get_barrier_semaphore()
-    greeted = 0
-    for off in range(n_sub):
-        peer = lax.rem(sub + off, n_sub)
-        for c in (above, below) + ((chan,) if off else ()):
-            pl.semaphore_signal(barrier, inc=1, device_id=(c, peer), device_id_type=MESH)
-            greeted += 1
-    for off in range(2, n_chan - 1):
-        pl.semaphore_signal(
-            barrier, inc=1, device_id=(lax.rem(chan + off, n_chan), sub), device_id_type=MESH
-        )
-        greeted += 1
-    pl.semaphore_wait(barrier, greeted)
 
     def copy_to(src, dst, send, recv, device):
         return pltpu.make_async_remote_copy(
@@ -404,67 +410,19 @@
 
     whole = pl.BlockSpec(memory_space=pltpu.VMEM)
     dma = pltpu.SemaphoreType.DMA
-    padded, prof = pl.pallas_call(
-        functools.partial(halo_kernel, nb, na, n_chan),
-        in_specs=[whole] * 2,
-        out_specs=[whole] * 2,
-        out_shape=[
-            jax.ShapeDtypeStruct((2, nb + 2 * na, LANES), F32),
-            jax.ShapeDtypeStruct((2, na, LANES, LANES), F32),
-        ],
-        scratch_shapes=[
-            pltpu.VMEM((2, harmonics), F32), pltpu.VMEM((2, harmonics), F32), dma((2,)), dma((2,)),
-        ],
-        compiler_params=pltpu.CompilerParams(collective_id=1, has_side_effects=True),
-    )(filter_init, profile_init)
     x = spectra.reshape(2, na, LANES, owned)
 
-    main, tail, head = pl.pallas_call(
-        functools.partial(gradient_kernel, nb, na, factor),
-        grid=(LANES // 32,),
-        in_specs=[
-            pl.BlockSpec((2, nb + 2 * na, LANES), lambda m: (0, 0, 0)),
-            pl.BlockSpec((2, na, 32, LANES), lambda m: (0, 0, m, 0)),
-            pl.BlockSpec((2, na, 32, owned), lambda m: (0, 0, m, 0)),
-        ],
-        out_specs=[
-            pl.BlockSpec((main_rows, LANES), lambda m: (0, 0)),
-            pl.BlockSpec((2 * na, LANES), lambda m: (0, 0)),
-            pl.BlockSpec((2 * na, LANES), lambda m: (0, 0)),
-        ],
-        out_shape=[
-            jax.ShapeDtypeStruct((main_rows, LANES), F32),
-            jax.ShapeDtypeStruct((2 * na, LANES), F32),
-            jax.ShapeDtypeStruct((2 * na, LANES), F32),
-        ],
-        scratch_shapes=[
-            pltpu.VMEM((2, ext, 8, LANES), F32),
-            pltpu.VMEM((2, ext, 8, LANES), F32),
-            pltpu.VMEM((2, ext, 16, LANES), F32),
-            pltpu.VMEM((2, ext, 16, LANES), F32),
-            pltpu.VMEM((2, ext, 16, LANES), F32),
-            pltpu.VMEM((2, ext, 16, LANES), F32),
-            pltpu.VMEM((2, ext, 16, LANES), F32),
-            pltpu.VMEM((2, ext, 16, LANES), F32),
-            pltpu.VMEM((2, ext, 16, LANES), F32),
-            pltpu.VMEM((2, ext, 16, LANES), F32),
-            pltpu.VMEM((2, ext, 8, LANES), F32),
-            pltpu.VMEM((2, ext, 8, LANES), F32),
-            pltpu.VMEM((2, na, LANES, LANES), F32),
-            pltpu.VMEM((16, LANES), F32),
-        ],
-    )(padded, prof, x)
-
-    step, prof_step, misfit = pl.pallas_call(
-        functools.partial(reduce_kernel, nb, na, n_chan, n_sub, harmonics, weight),
-        in_specs=[whole] * 3,
-        out_specs=[whole, whole, pl.BlockSpec(memory_space=pltpu.SMEM)],
-        out_shape=[
-            jax.ShapeDtypeStruct((2, owned), F32),
-            jax.ShapeDtypeStruct((2, harmonics), F32),
-            jax.ShapeDtypeStruct((1,), F32),
-        ],
-        scratch_shapes=[
+    strip = pltpu.VMEM((2, ext, 16, LANES), F32)
+    base = pltpu.VMEM((2, ext, 8, LANES), F32)
+    halo = pltpu.VMEM((2, harmonics), F32)
+    scratch = [
+        pltpu.VMEM((2, nb + 2 * na, LANES), F32),
+        pltpu.VMEM((2, na, LANES, LANES), F32),
+        halo, halo, dma((2,)), dma((2,)),
+        pltpu.VMEM((main_rows, LANES), F32),
+        pltpu.VMEM((2 * na, LANES), F32),
+        pltpu.VMEM((2 * na, LANES), F32),
+        [
             pltpu.VMEM((n_sub, main_rows, LANES), F32),
             pltpu.VMEM((n_sub, 2 * na, LANES), F32),
             pltpu.VMEM((n_sub, 2 * na, LANES), F32),
@@ -475,8 +433,27 @@
             dma((n_sub,)), dma((n_sub,)),
             dma((n_chan,)), dma((n_chan,)),
         ],
+        base, base, *([strip] * 8), base, base,
+        pltpu.VMEM((2, na, LANES, LANES), F32),
+        pltpu.VMEM((16, LANES), F32),
+    ]
+    step, prof_step, misfit = pl.pallas_call(
+        functools.partial(
+            gradient_kernel, nb, na, n_chan, n_sub, harmonics, weight, factor
+        ),
+        grid=(LANES // 32,),
+        in_specs=[
+            whole, whole, pl.BlockSpec((2, na, 32, owned), lambda m: (0, 0, m, 0)),
+        ],
+        out_specs=[whole, whole, pl.BlockSpec(memory_space=pltpu.SMEM)],
+        out_shape=[
+            jax.ShapeDtypeStruct((2, owned), F32),
+            jax.ShapeDtypeStruct((2, harmonics), F32),
+            jax.ShapeDtypeStruct((1,), F32),
+        ],
+        scratch_shapes=scratch,
         compiler_params=pltpu.CompilerParams(collective_id=0, has_side_effects=True),
-    )(main, tail, head)
+    )(filter_init, profile_init, x)
     return (filter_init - step, profile_init - prof_step, misfit)
 
 

time: 49.6 us -> 45.5 us (0.917)
  Pallas kernels: 44.2 us -> 40.2 us
    pallas_call x3 -> x1, Pallas kernels: 44.2 us -> 40.2 us  [on_device(): pl.pallas_call(functools.partial(gradient_kernel, nb, na, n_chan, n_sub,...]
where the time goes in v4:
time: 45.5 us; the launch traced here: 45.2 us
  Pallas kernels  40.2 us (88%)
  other arithmetic  2.67 us (6%)
  between operations  2.35 us (5%)
    pallas_call x1, Pallas kernels, on_device(): pl.pallas_call(functools.partial(gradient_kernel, nb, na, n_chan, n_sub,...  40.2 us
    sub x2, other arithmetic, on_device(): return (filter_init - step, profile_init - prof_step, misfit)  2.67 us

profile of v4, /device:TPU:0, one launch (start us, length us, event | category | flops | bytes accessed | tf_op | source)
XLA Modules:
  0.0 45.2 jit_solution(784199754036615521)
XLA Ops:
  0.6 0.0 copy-start.1
  0.6 0.0 copy-start
  0.7 40.2 %shard_map.58 = (f32[2,4096]{1,0:T(2,128)}, f32[2,512]{1,0:T(2,128)}, f32[1]{0:T(128)}) custom-call(f32[2,4096]{1,0:T(2,128)} %filter_ref.1, f32[2,512]{1,0:T(2,128)} %profile_ref.1, bf16[2,4,128,4096]{3,2,1,0:T(8,128)(2,1)} %bitcast.1), custom_call_target="tpu_custom_call" | custom-call | tf_op jit(solution)/shard_map/pallas_call | solution.py:440
  40.9 0.0 copy-done
  40.9 1.4 %sub.6 = f32[2,4096]{1,0:T(2,128)} subtract(f32[2,4096]{1,0:T(2,128)S(1)} %copy-done, f32[2,4096]{1,0:T(2,128)} %get-tuple-element.6) | non-fusion elementwise | flops 8192 | bytes 98304 | tf_op jit(solution)/shard_map/sub | solution.py:457
  42.3 0.0 copy-done.1
  42.3 1.3 %sub.7 = f32[2,512]{1,0:T(2,128)} subtract(f32[2,512]{1,0:T(2,128)S(1)} %copy-done.1, f32[2,512]{1,0:T(2,128)} %get-tuple-element.7) | non-fusion elementwise | flops 1024 | bytes 12288 | tf_op jit(solution)/shard_map/sub | solution.py:457
Async XLA Ops:
  0.6 41.6 %copy-start.1 = (f32[2,512]{1,0:T(2,128)S(1)}, f32[2,512]{1,0:T(2,128)}, u32[]{:S(2)}) copy-start(f32[2,512]{1,0:T(2,128)} %profile_ref.1) | copy-start | bytes 12292
  0.6 40.2 %copy-start = (f32[2,4096]{1,0:T(2,128)S(1)}, f32[2,4096]{1,0:T(2,128)}, u32[]{:S(2)}) copy-start(f32[2,4096]{1,0:T(2,128)} %filter_ref.1) | copy-start | bytes 98308
